TPU v7x, 128 devices: a whole 4x4x4 slice. The times are simulated.
128 devices in a mesh: row: 8 (over z, x_lo), col: 16 (over x_hi, y, core).
Axes of the slice: x: 4 (x_hi: 2, x_lo: 2; x = x_hi * 2 + x_lo), y: 4, z: 4, core: 2. Of those that a mesh axis runs over, the one named last changes fastest.
Arguments:
- right_side: float32 [3, 24576], P(None, ('row', 'col'))
- linewidth: float32 [24576], P(('row', 'col')), may hold values from 0.6 to 2.4
- scattering: float32 [24576, 24576], P('row', 'col'), as said below
Outputs:
- solution: float32 [3, 24576], P(None, ('row', 'col'))
- residual: float32 [3, 24576], P(None, ('row', 'col'))
Inputs may be any that keep to these rules, and one draw needn't show every extreme that they name: scattering is symmetric.
All inputs are finite; a program needn't handle non-finite values.
Results may differ from a plain program's by a relative error of at most 0.00018.
Values sent between devices are 32-bit elements; how exact they have to be, the bound alone decides.
A program may use at most 64 MiB of HBM per device.

v0:
```python
import functools

import jax
import jax.numpy as jnp
from jax import lax
from jax.sharding import Mesh
from jax.sharding import PartitionSpec as P

ITERS = 2
COL = ("col_0", "col_1", "col_2")
ROW = ("row_0", "row_1")
ROW_COL = ("row_0", "row_1", "col_0", "col_1", "col_2")


def joined_along(pieces, dim):
    pieces = jnp.moveaxis(pieces, 0, dim)
    shape = pieces.shape
    return pieces.reshape(*shape[:dim], shape[dim] * shape[dim + 1], *shape[dim + 2 :])


def copy_for_each(shard, axis):
    copies = jnp.broadcast_to(shard, (lax.axis_size(axis), *shard.shape))
    return lax.all_to_all(copies, axis, split_axis=0, concat_axis=0, tiled=True)


def collect(shard, axis, dim):
    return joined_along(copy_for_each(shard, axis), dim)


def from_root(shard, axis, root):
    return lax.dynamic_index_in_dim(lax.all_gather(shard, axis), root, 0, keepdims=False)


def in_blocks(shard, dim, peers):
    shape = shard.shape
    pieces = shard.reshape(*shape[:dim], peers, shape[dim] // peers, *shape[dim + 1 :])
    return jnp.moveaxis(pieces, dim, 0)


def sent_and_summed(shard, axis, dim):
    pieces = in_blocks(shard, dim, lax.axis_size(axis))
    arrived = lax.all_to_all(pieces, axis, split_axis=0, concat_axis=0, tiled=True)
    return arrived.sum(axis=0)


def over_axes(shard, axes):
    return functools.reduce(lax.psum, axes, shard)


def apply_operator(vectors, linewidth, scattering):
    block_cols = scattering.shape[1]
    column_index = lax.axis_index(COL)
    per_row = lax.axis_size(COL) // lax.axis_size(ROW)
    own_rows = collect(vectors, COL, 1)
    owner_row = column_index // per_row
    owned = from_root(own_rows, ROW, owner_row)
    columns = lax.dynamic_slice_in_dim(owned, column_index % per_row * block_cols, block_cols, 1)
    partial_terms = lax.dot_general(
        columns,
        scattering,
        (((1,), (1,)), ((), ())),
        precision=lax.Precision.HIGHEST,
        preferred_element_type=jnp.float32,
    )
    summed = sent_and_summed(partial_terms, COL, 1)
    return linewidth[None, :] * vectors + summed


def two_products(residual, image):
    return (
        over_axes(jnp.sum(residual * residual, axis=1), ROW_COL),
        over_axes(jnp.sum(residual * image, axis=1), ROW_COL),
    )


def body(right_side, linewidth, scattering):
    solution = jnp.zeros_like(right_side)
    residual = right_side
    image = apply_operator(residual, linewidth, scattering)
    norm_now, product = two_products(residual, image)
    step_size = norm_now / product
    direction = residual
    along = image
    for iteration in range(ITERS):
        solution = solution + step_size[:, None] * direction
        residual = residual - step_size[:, None] * along
        if iteration + 1 < ITERS:
            image = apply_operator(residual, linewidth, scattering)
            norm_next, product = two_products(residual, image)
            factor = norm_next / norm_now
            step_size = norm_next / (product - factor * norm_next / step_size)
            direction = residual + factor[:, None] * direction
            along = image + factor[:, None] * along
            norm_now = norm_next
    return (solution, residual)


def solution(mesh):
    torus = Mesh(mesh.devices.reshape(4, 2, 2, 4, 2), ("row_0", "row_1", "col_0", "col_1", "col_2"))
    return jax.shard_map(
        body,
        mesh=torus,
        in_specs=(P(None, ROW_COL), P(ROW_COL), P(ROW, COL)),
        out_specs=(P(None, ROW_COL), P(None, ROW_COL)),
        check_vma=False,
    )
```

profile of v0, /device:TPU:1, one launch (start us, length us, event | category | flops | bytes accessed | tf_op | source)
XLA Modules:
  0.0 209.4 jit_solution(10302966817756073051)
XLA Ops:
  0.6 1.4 broadcast_in_dim.4
  2.0 8.4 %all-to-all-start = ((f32[16,3,192]{2,1,0:T(4,128)}), f32[16,3,192]{2,1,0:T(4,128)S(1)}, u32[]{:S(2)}, u32[]{:S(2)}) async-start(f32[16,3,192]{2,1,0:T(4,128)} %broadcast_in_dim.4), calls=%async_computation | async-start | bytes 131072 | tf_op jit(solution)/shard_map/all_to_all | solution.py:23
  10.5 7.3 %all-to-all-done = f32[16,3,192]{2,1,0:T(4,128)S(1)} async-done(((f32[16,3,192]{2,1,0:T(4,128)}), f32[16,3,192]{2,1,0:T(4,128)S(1)}, u32[]{:S(2)}, u32[]{:S(2)}) %all-to-all-start) | async-done | bytes 36896 | tf_op jit(solution)/shard_map/all_to_all | solution.py:23
  17.8 0.1 all_gather_reshape.6
  17.9 25.0 %all_gather.6 = f32[8,3,3072]{2,1,0:T(4,128)S(1)} all-gather(f32[1,3,3072]{2,1,0:T(4,128)S(1)} %all_gather_reshape.6), channel_id=1, replica_groups=mesh['row_0'=4,'row_1'=2,'col_0'=2,'col_1'=4,'col_2'=2] {'row_0','row_1'}, dimensions={0}, use_global_device_ids=true | all-gather | bytes 331776 | tf_op jit(solution)/shard_map/all_gather | solution.py:31
  42.9 18.2 %convolution_bitcast_fusion.1 = f32[16,3,192]{2,1,0:T(4,128)S(1)} fusion(f32[16,192,1536]{2,1,0:T(8,128)} %bitcast.17, f32[8,3,3072]{2,1,0:T(4,128)S(1)} %all_gather.6, s32[]{:T(128)S(6)} %select_n.29, s32[]{:T(128)S(6)} %select_n.32), kind=kOutput, calls=%fused_computation.1 | convolution fusion | flops 169869312 | bytes 18935816 | tf_op jit(solution)/shard_map/dot_general | solution.py:58
  61.1 16.2 %all_to_all.20 = f32[16,3,192]{2,1,0:T(4,128)S(1)} all-to-all(f32[16,3,192]{2,1,0:T(4,128)S(1)} %convolution_bitcast_fusion.1), channel_id=1, replica_groups=mesh['row_0'=4,'row_1'=2,'col_0'=2,'col_1'=4,'col_2'=2] {'col_0','col_1'..., dimensions={0} | all-to-all | bytes 73728 | tf_op jit(solution)/shard_map/all_to_all | solution.py:42
  77.3 0.1 multiply_reduce_fusion.2
  77.5 6.3 %all-reduce.3 = (f32[3]{0:T(128)S(1)}, f32[3]{0:T(128)S(1)}) all-reduce(f32[3]{0:T(128)S(1)} %get-tuple-element.5, f32[3]{0:T(128)S(1)} %get-tuple-element.4), channel_id=1, replica_groups=mesh['row_0'=4,'row_1'=2,'col_0'=2,'col_1'=4,'col_2'=2] {'row_0'}, use_global_device_ids=true, to_apply=%region_1.2 | all-reduce | flops 6 | bytes 48 | tf_op jit(solution)/shard_map/psum | solution.py:47
  83.8 4.6 %all-reduce.9 = (f32[3]{0:T(128)S(1)}, f32[3]{0:T(128)S(1)}) all-reduce(f32[3]{0:T(128)S(1)} %get-tuple-element.12, f32[3]{0:T(128)S(1)} %get-tuple-element.13), channel_id=1, replica_groups=mesh['row_0'=4,'row_1'=2,'col_0'=2,'col_1'=4,'col_2'=2] {'row_1'}, use_global_device_ids=true, to_apply=%region_2.3 | all-reduce | flops 6 | bytes 48 | tf_op jit(solution)/shard_map/psum | solution.py:47
  88.4 5.3 %all-reduce.7 = (f32[3]{0:T(128)S(1)}, f32[3]{0:T(128)S(1)}) all-reduce(f32[3]{0:T(128)S(1)} %get-tuple-element.24, f32[3]{0:T(128)S(1)} %get-tuple-element.25), channel_id=1, replica_groups=mesh['row_0'=4,'row_1'=2,'col_0'=2,'col_1'=4,'col_2'=2] {'col_0'}, use_global_device_ids=true, to_apply=%region_3.4 | all-reduce | flops 6 | bytes 48 | tf_op jit(solution)/shard_map/psum | solution.py:47
  93.6 7.0 %all-reduce.1 = (f32[3]{0:T(128)S(1)}, f32[3]{0:T(128)S(1)}) all-reduce(f32[3]{0:T(128)S(1)} %get-tuple-element.20, f32[3]{0:T(128)S(1)} %get-tuple-element.21), channel_id=1, replica_groups=mesh['row_0'=4,'row_1'=2,'col_0'=2,'col_1'=4,'col_2'=2] {'col_1'}, use_global_device_ids=true, to_apply=%region_4.5 | all-reduce | flops 6 | bytes 48 | tf_op jit(solution)/shard_map/psum | solution.py:47
  100.6 8.6 %all-reduce.5 = (f32[3]{0:T(128)S(1)}, f32[3]{0:T(128)S(1)}) all-reduce(f32[3]{0:T(128)S(1)} %get-tuple-element.8, f32[3]{0:T(128)S(1)} %get-tuple-element.9), channel_id=1, replica_groups=mesh['row_0'=4,'row_1'=2,'col_0'=2,'col_1'=4,'col_2'=2] {'col_2'}, use_global_device_ids=true, to_apply=%region_5.6 | all-reduce | flops 6 | bytes 48 | tf_op jit(solution)/shard_map/psum | solution.py:47
  109.3 10.2 %all_to_all.21 = f32[16,3,192]{2,1,0:T(4,128)S(1)} all-to-all(f32[16,3,192]{2,1,0:T(4,128)S(1)} %broadcast_in_dim.5), channel_id=1, replica_groups=mesh['row_0'=4,'row_1'=2,'col_0'=2,'col_1'=4,'col_2'=2] {'col_0','col_1'..., dimensions={0} | all-to-all | bytes 73728 | tf_op jit(solution)/shard_map/all_to_all | solution.py:23
  119.5 24.1 %all_gather.7 = f32[8,3,3072]{2,1,0:T(4,128)S(1)} all-gather(f32[1,3,3072]{2,1,0:T(4,128)S(1)} %all_gather_reshape.7), channel_id=1, replica_groups=mesh['row_0'=4,'row_1'=2,'col_0'=2,'col_1'=4,'col_2'=2] {'row_0','row_1'}, dimensions={0}, use_global_device_ids=true | all-gather | bytes 331776 | tf_op jit(solution)/shard_map/all_gather | solution.py:31
  143.7 18.2 %convolution_bitcast_fusion = f32[16,3,192]{2,1,0:T(4,128)S(1)} fusion(f32[16,192,1536]{2,1,0:T(8,128)} %bitcast.18, f32[8,3,3072]{2,1,0:T(4,128)S(1)} %all_gather.7, s32[]{:T(128)S(6)} %select_n.29, s32[]{:T(128)S(6)} %select_n.32), kind=kOutput, calls=%fused_computation | convolution fusion | flops 169869312 | bytes 18935816 | tf_op jit(solution)/shard_map/dot_general | solution.py:58
  161.9 15.4 %all_to_all.22 = f32[16,3,192]{2,1,0:T(4,128)S(1)} all-to-all(f32[16,3,192]{2,1,0:T(4,128)S(1)} %convolution_bitcast_fusion), channel_id=1, replica_groups=mesh['row_0'=4,'row_1'=2,'col_0'=2,'col_1'=4,'col_2'=2] {'col_0','col_1'..., dimensions={0} | all-to-all | bytes 73728 | tf_op jit(solution)/shard_map/all_to_all | solution.py:42
  177.3 0.1 multiply_reduce_fusion
  177.5 6.3 %all-reduce.2 = (f32[3]{0:T(128)S(1)}, f32[3]{0:T(128)S(1)}) all-reduce(f32[3]{0:T(128)S(1)} %get-tuple-element.3, f32[3]{0:T(128)S(1)} %get-tuple-element.2), channel_id=1, replica_groups=mesh['row_0'=4,'row_1'=2,'col_0'=2,'col_1'=4,'col_2'=2] {'row_0'}, use_global_device_ids=true, to_apply=%region_14.15 | all-reduce | flops 6 | bytes 48 | tf_op jit(solution)/shard_map/psum | solution.py:47
  183.8 4.1 %all-reduce.8 = (f32[3]{0:T(128)S(1)}, f32[3]{0:T(128)S(1)}) all-reduce(f32[3]{0:T(128)S(1)} %get-tuple-element.10, f32[3]{0:T(128)S(1)} %get-tuple-element.11), channel_id=1, replica_groups=mesh['row_0'=4,'row_1'=2,'col_0'=2,'col_1'=4,'col_2'=2] {'row_1'}, use_global_device_ids=true, to_apply=%region_15.16 | all-reduce | flops 6 | bytes 48 | tf_op jit(solution)/shard_map/psum | solution.py:47
  188.0 5.3 %all-reduce.6 = (f32[3]{0:T(128)S(1)}, f32[3]{0:T(128)S(1)}) all-reduce(f32[3]{0:T(128)S(1)} %get-tuple-element.22, f32[3]{0:T(128)S(1)} %get-tuple-element.23), channel_id=1, replica_groups=mesh['row_0'=4,'row_1'=2,'col_0'=2,'col_1'=4,'col_2'=2] {'col_0'}, use_global_device_ids=true, to_apply=%region_16.17 | all-reduce | flops 6 | bytes 48 | tf_op jit(solution)/shard_map/psum | solution.py:47
  193.2 7.0 %all-reduce = (f32[3]{0:T(128)S(1)}, f32[3]{0:T(128)S(1)}) all-reduce(f32[3]{0:T(128)S(1)} %get-tuple-element.18, f32[3]{0:T(128)S(1)} %get-tuple-element.19), channel_id=1, replica_groups=mesh['row_0'=4,'row_1'=2,'col_0'=2,'col_1'=4,'col_2'=2] {'col_1'}, use_global_device_ids=true, to_apply=%region_17.18 | all-reduce | flops 6 | bytes 48 | tf_op jit(solution)/shard_map/psum | solution.py:47
  200.2 8.6 %all-reduce.4 = (f32[3]{0:T(128)S(1)}, f32[3]{0:T(128)S(1)}) all-reduce(f32[3]{0:T(128)S(1)} %get-tuple-element.6, f32[3]{0:T(128)S(1)} %get-tuple-element.7), channel_id=1, replica_groups=mesh['row_0'=4,'row_1'=2,'col_0'=2,'col_1'=4,'col_2'=2] {'col_2'}, use_global_device_ids=true, to_apply=%region_18.19 | all-reduce | flops 6 | bytes 48 | tf_op jit(solution)/shard_map/psum | solution.py:47
  208.8 0.7 multiply_subtract_fusion
  (13 shorter events, 0.3 us)
Async XLA Ops:
  0.6 76.7 %copy-start = (f32[3,192]{1,0:T(4,128)S(1)}, f32[3,192]{1,0:T(4,128)}, u32[]{:S(2)}) copy-start(f32[3,192]{1,0:T(4,128)} %param.3) | copy-start | bytes 6916
  0.6 76.7 %copy-start.1 = (f32[192]{0:T(256)S(1)}, f32[192]{0:T(256)}, u32[]{:S(2)}) copy-start(f32[192]{0:T(256)} %param.4) | copy-start | bytes 2308
  2.0 15.8 %all-to-all-start = ((f32[16,3,192]{2,1,0:T(4,128)}), f32[16,3,192]{2,1,0:T(4,128)S(1)}, u32[]{:S(2)}, u32[]{:S(2)}) async-start(f32[16,3,192]{2,1,0:T(4,128)} %broadcast_in_dim.4), calls=%async_computation | async-start | bytes 131072 | tf_op jit(solution)/shard_map/all_to_all | solution.py:23
where the time goes:
time: 210 us; the launch traced here: 209 us
  blocking collectives  154 us (73%)
  matrix products  36.5 us (17%)
  starting transfers between devices  8.45 us (4%)
  waiting for transfers between devices  7.33 us (3%)
    psum x10, blocking collectives, over_axes(): return functools.reduce(lax.psum, axes, shard)  62.9 us
    all_gather x2, blocking collectives, from_root(): lax.all_gather(shard, axis)  49.1 us
    dot_general x2, matrix products, apply_operator(): lax.dot_general(columns, scattering, (((1,), (1,)), ((), ())), precision=...  36.5 us
    all_to_all x2, blocking collectives, sent_and_summed(): lax.all_to_all(pieces, axis, split_axis=0, concat_axis=0, tiled=True)  31.6 us
    all_to_all x1, blocking collectives, copy_for_each(): return lax.all_to_all(copies, axis, split_axis=0, concat_axis=0, tiled=True)  10.2 us
    all_to_all x1, starting transfers between devices, copy_for_each(): return lax.all_to_all(copies, axis, split_axis=0, concat_axis=0, tiled=True)  8.45 us
    all_to_all x1, waiting for transfers between devices, copy_for_each(): return lax.all_to_all(copies, axis, split_axis=0, concat_axis=0, tiled=True)  7.33 us
  transfers between devices with their start and end apart: 1, of which 1 were waited for; matrix products, arithmetic and copies ran while one was open for 0% of the time, Pallas kernels for 0%

commit v1 on v0

v1 whole, which is shorter than its diff:
```python
import functools

import jax
import jax.numpy as jnp
from jax import lax
from jax.experimental import pallas as pl
from jax.experimental.pallas import tpu as pltpu
from jax.sharding import PartitionSpec as P

ROW_COL = ("row", "col")
MESH = pl.DeviceIdType.MESH
F32, BF16 = jnp.float32, jnp.bfloat16
PAD = 256


def three_parts(rows):
    top = rows.astype(BF16).astype(F32)
    rest = rows - top
    middle = rest.astype(BF16).astype(F32)
    low = rest - middle
    return jnp.concatenate([top, middle, low, jnp.zeros_like(low)], axis=0).astype(BF16)


def joined(product):
    return product[0:4] + product[4:8] + product[8:12]


def await_bytes(ref, count, sem):
    part = ref.at[pl.ds(0, count)]
    pltpu.make_async_copy(part, part, sem).wait()


def kernel(rows_n, cols_n, b_ref, width_ref, s_hbm, x_ref, res_ref,
           s_f32, s_hi, s_lo, a_slot, v_buf, p_slot, w_buf, own_w, q_buf, d_slot, e_slot,
           s_sem, send_sem, recv_sem, own_sem):
    row, col = lax.axis_index("row"), lax.axis_index("col")
    me = row * cols_n + col
    block_rows, block_cols = s_f32.shape
    modes = b_ref.shape[1]
    chunk = modes
    chunks = block_rows // chunk
    odd = lax.rem(col, 2)

    def load(i):
        at = pl.ds(pl.multiple_of(i * chunk, chunk), chunk)
        return pltpu.make_async_copy(s_hbm.at[at], s_f32.at[at], s_sem.at[i])

    def start_load(i, _):
        load(i).start()
        return 0

    lax.fori_loop(0, chunks, start_load, 0)

    row_peers = [(row, lax.rem(col + i, cols_n)) for i in range(1, cols_n)]
    col_peers = [(lax.rem(row + i, rows_n), col) for i in range(1, rows_n)]
    barrier = pltpu.get_barrier_semaphore()
    for peer in row_peers + col_peers:
        pl.semaphore_signal(barrier, inc=1, device_id=peer, device_id_type=MESH)

    lanes = lax.broadcasted_iota(jnp.int32, (4, PAD), 1)
    shift = odd * (PAD - modes)
    mine = (lanes >= shift) & (lanes < shift + modes)
    fresh = jnp.concatenate([b_ref[...], width_ref[...]], axis=0)
    fresh = jnp.concatenate([fresh, jnp.zeros((4, PAD - modes), F32)], axis=1)
    own_b = jnp.where(odd == 1, pltpu.roll(fresh, PAD - modes, 1), fresh)
    a_slot[col] = own_b
    pl.semaphore_wait(barrier, rows_n + cols_n - 2)

    def send(src, dst, peer, at):
        copy = pltpu.make_async_remote_copy(
            src_ref=src, dst_ref=dst, send_sem=send_sem.at[at], recv_sem=recv_sem.at[at],
            device_id=peer, device_id_type=MESH)
        copy.start()

    for peer in row_peers:
        send(a_slot.at[col], a_slot.at[col], peer, 0)

    step = 32

    def split_chunk(i, _):
        load(i).wait()

        def split(k, _):
            at = pl.ds(pl.multiple_of(i * chunk + k * step, step), step)
            whole = s_f32[at]
            high = whole.astype(BF16)
            s_hi[at] = high
            s_lo[at] = (whole - high.astype(F32)).astype(BF16)
            return 0

        return lax.fori_loop(0, chunk // step, split, 0)

    lax.fori_loop(0, chunks, split_chunk, 0)

    await_bytes(a_slot, cols_n - 1, recv_sem.at[0])
    pieces = []
    for pair in range(cols_n // 2):
        left, right = a_slot[2 * pair], a_slot[2 * pair + 1]
        pieces += [left[:, :128], left[:, 128:] + right[:, :128], right[:, 128:]]
    vector = jnp.concatenate(pieces, axis=1)
    v_buf[...] = vector

    depth = 512
    v_parts = three_parts(vector)
    w_in = w_buf
    total = jnp.zeros((16, block_cols), F32)
    for k in range(block_rows // depth):
        part = v_parts[:, k * depth:(k + 1) * depth]
        at = pl.ds(k * depth, depth)
        total = total + jnp.dot(part, s_hi[at], preferred_element_type=F32)
        total = total + jnp.dot(part, s_lo[at], preferred_element_type=F32)
    on_diagonal = row == col // 2
    half = v_buf[:, pl.ds(pl.multiple_of(odd * block_cols, 128), block_cols)]
    flag = jnp.where(on_diagonal, 1.0, 0.0).astype(F32)
    p_slot[row] = joined(total) + half * half[3:4] * flag
    for peer in col_peers:
        send(p_slot.at[row], p_slot.at[row], peer, 1)
    await_bytes(p_slot, rows_n - 1, recv_sem.at[1])
    w1 = p_slot[0]
    for i in range(1, rows_n):
        w1 = w1 + p_slot[i]
    w_in[...] = w1

    per_block = block_cols // modes

    def window(j):
        return pl.ds(pl.multiple_of((j // 2) * (2 * modes) + lax.rem(j, 2) * 128, 128), PAD)

    @pl.when(on_diagonal)
    def _():
        def give(j, _):
            to = odd * per_block + j

            @pl.when(to != col)
            def _():
                pltpu.make_async_remote_copy(
                    src_ref=w_buf.at[:, window(j)], dst_ref=own_w, send_sem=own_sem.at[0], recv_sem=own_sem.at[1],
                    device_id=(row, to), device_id_type=MESH).start()

            @pl.when(to == col)
            def _():
                own_w[...] = w_buf[:, window(j)]

            return 0

        lax.fori_loop(0, per_block, give, 0)

    w_parts = three_parts(w1)
    width = 2 * modes

    def second(i, _):
        at = pl.ds(pl.multiple_of(i * width, width), width)
        dims = (((1,), (1,)), ((), ()))
        out = lax.dot_general(w_parts, s_hi[at], dims, preferred_element_type=F32)
        out = out + lax.dot_general(w_parts, s_lo[at], dims, preferred_element_type=F32)
        q_buf[:, at] = joined(out)
        for j in range(2):
            to = 2 * i + j

            @pl.when(to != col)
            def _():
                send(q_buf.at[:, window(to)], d_slot.at[col], (row, to), 2)

        return 0

    lax.fori_loop(0, block_rows // width, second, 0)
    d_slot[col] = q_buf[:, window(col)]

    giver = 2 * row + col // per_block
    @pl.when(giver != col)
    def _():
        pltpu.make_async_copy(own_w, own_w, own_sem.at[1]).wait()

    await_bytes(d_slot, cols_n - 1, recv_sem.at[2])
    own_w1 = jnp.where(mine, own_w[...], 0.0)
    w2 = d_slot[0]
    for i in range(1, cols_n):
        w2 = w2 + d_slot[i]
    own_w2 = jnp.where(mine, w2, 0.0) + own_b[3:4] * own_w1

    def inner(u, v):
        return jnp.sum(u * v, axis=1, keepdims=True)

    lane = lax.broadcasted_iota(jnp.int32, (4, 128), 1)
    moments = jnp.where(lane == 0, inner(own_b, own_b),
              jnp.where(lane == 1, inner(own_b, own_w1),
              jnp.where(lane == 2, inner(own_w1, own_w1), inner(own_w1, own_w2))))
    e_slot[me] = moments
    n = rows_n * cols_n

    def tell(i, _):
        to = lax.rem(me + i, n)
        send(e_slot.at[me], e_slot.at[me], (to // cols_n, lax.rem(to, cols_n)), 3)
        return 0

    lax.fori_loop(1, n, tell, 0, unroll=8)
    await_bytes(e_slot, n - 1, recv_sem.at[3])
    g = jnp.sum(e_slot[...], axis=0)
    g0, g1, g2, g3 = (g[:, i:i + 1] for i in range(4))
    a0 = g0 / g1
    norm = g0 - 2.0 * a0 * g1 + a0 * a0 * g2
    beta = norm / g0
    more = 1.0 + beta
    a1 = norm / (more * more * g1 - 2.0 * more * a0 * g2 + a0 * a0 * g3)
    r1 = own_b - a0 * own_w1
    x2 = a0 * own_b + a1 * (r1 + beta * own_b)
    r2 = r1 - a1 * (more * own_w1 - a0 * own_w2)
    x2 = jnp.where(odd == 1, pltpu.roll(x2, modes, 1), x2)
    r2 = jnp.where(odd == 1, pltpu.roll(r2, modes, 1), r2)
    x_ref[...] = x2[0:3, :modes]
    res_ref[...] = r2[0:3, :modes]

    await_bytes(a_slot, cols_n - 1, send_sem.at[0])
    await_bytes(p_slot, rows_n - 1, send_sem.at[1])
    await_bytes(d_slot, cols_n - 1, send_sem.at[2])
    await_bytes(e_slot, n - 1, send_sem.at[3])

    @pl.when(on_diagonal)
    def _():
        def sent(j, _):
            @pl.when(odd * per_block + j != col)
            def _():
                pltpu.make_async_copy(own_w, own_w, own_sem.at[0]).wait()

            return 0

        lax.fori_loop(0, per_block, sent, 0)


def solution(mesh):
    rows_n, cols_n = mesh.shape["row"], mesh.shape["col"]
    n = rows_n * cols_n

    def body(right_side, linewidth, scattering):
        block_rows, block_cols = scattering.shape
        vmem = pl.BlockSpec(memory_space=pltpu.VMEM)
        out = jax.ShapeDtypeStruct(right_side.shape, F32)
        return pl.pallas_call(
            functools.partial(kernel, rows_n, cols_n),
            out_shape=(out, out),
            in_specs=[vmem, vmem, pl.BlockSpec(memory_space=pl.ANY)],
            out_specs=(vmem, vmem),
            scratch_shapes=[
                pltpu.VMEM((block_rows, block_cols), F32),
                pltpu.VMEM((block_rows, block_cols), BF16),
                pltpu.VMEM((block_rows, block_cols), BF16),
                pltpu.VMEM((cols_n, 4, PAD), F32),
                pltpu.VMEM((4, block_rows), F32),
                pltpu.VMEM((rows_n, 4, block_cols), F32),
                pltpu.VMEM((4, block_cols), F32),
                pltpu.VMEM((4, PAD), F32),
                pltpu.VMEM((4, block_rows), F32),
                pltpu.VMEM((cols_n, 4, PAD), F32),
                pltpu.VMEM((n, 4, 128), F32),
                pltpu.SemaphoreType.DMA((cols_n,)),
                pltpu.SemaphoreType.DMA((4,)),
                pltpu.SemaphoreType.DMA((4,)),
                pltpu.SemaphoreType.DMA((2,)),
            ],
            compiler_params=pltpu.CompilerParams(
                collective_id=0, has_side_effects=True, vmem_limit_bytes=60 << 20),
        )(right_side, linewidth.reshape(1, -1), scattering)

    return jax.shard_map(
        body,
        mesh=mesh,
        in_specs=(P(None, ROW_COL), P(ROW_COL), P("row", "col")),
        out_specs=(P(None, ROW_COL), P(None, ROW_COL)),
        check_vma=False,
    )
```

time: 210 us -> 43.4 us (0.21)
  blocking collectives: 154 us -> 0 us
  Pallas kernels: 0 us -> 40 us
  matrix products: 36.5 us -> 0 us
  starting transfers between devices: 8.45 us -> 0 us
  waiting for transfers between devices: 7.33 us -> 0 us
    psum x10 -> x0, blocking collectives: 62.9 us -> none  [over_axes(): return functools.reduce(lax.psum, axes, shard)]
    all_gather x2 -> x0, blocking collectives: 49.1 us -> none  [from_root(): lax.all_gather(shard, axis)]
    all_to_all x3 -> x0, blocking collectives: 41.8 us -> none  [the longest x2 31.6 us: sent_and_summed(): lax.all_to_all(pieces, axis, split_axis=0, concat_axis=0, tiled=True)]
    pallas_call x0 -> x1, Pallas kernels: none -> 40 us  [body(): pl.pallas_call(functools.partial(kernel, rows_n, cols_n), out_shape=(out,...]
    dot_general x2 -> x0, matrix products: 36.5 us -> none  [apply_operator(): lax.dot_general(columns, scattering, (((1,), (1,)), ((), ())), precision=...]
    all_to_all x1 -> x0, starting transfers between devices: 8.45 us -> none  [copy_for_each(): return lax.all_to_all(copies, axis, split_axis=0, concat_axis=0, tiled=True)]
    all_to_all x1 -> x0, waiting for transfers between devices: 7.33 us -> none  [copy_for_each(): return lax.all_to_all(copies, axis, split_axis=0, concat_axis=0, tiled=True)]
    unnamed x4 -> x2, local copies, waits for them, and re-layouts: 0.01 us -> 2.53 us
  transfers between devices with their start and end apart: 1 -> 0, of which waited for: 1 -> 0; matrix products, arithmetic and copies ran while one was open for 0% -> 0% of each run, Pallas kernels for 0% -> 0%
where the time goes in v1:
time: 43.4 us; the launch traced here: 43.2 us
  Pallas kernels  40 us (92%)
  local copies, waits for them, and re-layouts  2.53 us (6%)
  between operations  0.64 us (1%)
    pallas_call x1, Pallas kernels, body(): pl.pallas_call(functools.partial(kernel, rows_n, cols_n), out_shape=(out,...  40 us
    unnamed x2, local copies, waits for them, and re-layouts  2.53 us

profile of v1, /device:TPU:1, one launch (start us, length us, event | category | flops | bytes accessed | tf_op | source)
XLA Modules:
  0.0 43.2 jit_solution(5685275890537341576)
XLA Ops:
  0.6 40.0 %shard_map.50 = (f32[3,192]{1,0:T(4,128)}, f32[3,192]{1,0:T(4,128)}) custom-call(f32[3,192]{1,0:T(4,128)} %b_ref.1, f32[1,192]{1,0:T(1,128)} %bitcast.1, f32[3072,1536]{1,0:T(8,128)} %s_hbm.1), custom_call_target="tpu_custom_call" | custom-call | tf_op jit(solution)/shard_map/pallas_call | solution.py:238
  40.7 1.3 %copy.7 = f32[3,192]{1,0:T(4,128)} copy(f32[3,192]{1,0:T(4,128)} %get-tuple-element.4) | data formatting | bytes 4608
  41.9 1.3 %copy.8 = f32[3,192]{1,0:T(4,128)} copy(f32[3,192]{1,0:T(4,128)} %get-tuple-element.5) | data formatting | bytes 4608

commit v2 on v1

v2 whole, which is shorter than its diff:
```python
import functools

import jax
import jax.numpy as jnp
from jax import lax
from jax.experimental import pallas as pl
from jax.experimental.pallas import tpu as pltpu
from jax.sharding import PartitionSpec as P

ROW_COL = ("row", "col")
MESH = pl.DeviceIdType.MESH
F32, BF16 = jnp.float32, jnp.bfloat16
LANES = 128
PAD = 2 * LANES


def three_parts(rows):
    top = rows.astype(BF16).astype(F32)
    rest = rows - top
    middle = rest.astype(BF16).astype(F32)
    low = rest - middle
    return jnp.concatenate([top, middle, low, jnp.zeros_like(low)], axis=0).astype(BF16)


def joined(product):
    return product[0:4] + product[4:8] + product[8:12]


def await_bytes(ref, count, sem):
    part = ref.at[pl.ds(0, count)]
    pltpu.make_async_copy(part, part, sem).wait()


def ring(d):
    return min(d, 4 - d)


def farthest_first(offsets):
    hops = lambda o: ring(o[0]) + ring(o[1]) + ring(o[2]) + 0.1 * o[3]
    return sorted((o for o in offsets if any(o)), key=lambda o: -hops(o))


def far_fourth(j):
    return 2 - j + 3 * (j // 2) - 2 * ((j + 1) // 4)


def kernel(rows_n, cols_n, b_hbm, width_hbm, s_hbm, x_part, res_part, res_step,
           s_f32, s_hi, s_lo, t_hi, t_lo, b_in, width_in, a_slot, v_buf, p_slot, w_buf, f_slot, q_buf,
           d_slot, e_slot, s_sem, in_sem, a_sem, send_sem, recv_sem):
    row, col = lax.axis_index("row"), lax.axis_index("col")
    me = row * cols_n + col
    block_rows, block_cols = s_f32.shape
    modes = b_in.shape[1]
    chips = cols_n // 2
    width = 2 * modes
    odd = col % 2

    z, x_lo, x_hi, y = row // 2, row % 2, col // 8, (col // 2) % 4
    x = x_hi * 2 + x_lo
    z_at = [((z + d) % 4) * 2 for d in range(4)]
    y_at = [((y + d) % 4) * 2 for d in range(4)]
    x_row = [((x + d) % 4) % 2 for d in range(4)]
    x_col = [((x + d) % 4) // 2 * 8 for d in range(4)]
    core_at = [odd, 1 - odd]

    def device(offset):
        dz, dy, dx, dc = offset
        return (z_at[dz] + x_row[dx], x_col[dx] + y_at[dy] + core_at[dc])

    def col_device(offset):
        dz, _, dx, _ = offset
        return (z_at[dz] + (row + dx) % 2, col)

    row_peers = [device(o) for o in farthest_first([(0, dy, dx, dc) for dy in range(4) for dx in (0, 2) for dc in (0, 1)])]
    col_peers = [col_device(o) for o in farthest_first([(dz, 0, dx, 0) for dz in range(4) for dx in (0, 1)])]
    everyone = [device(o) for o in farthest_first(
        [(dz, dy, dx, dc) for dz in range(4) for dy in range(4) for dx in range(4) for dc in (0, 1)])]

    small = [pltpu.make_async_copy(b_hbm, b_in, in_sem.at[0]), pltpu.make_async_copy(width_hbm, width_in, in_sem.at[1])]
    for copy in small:
        copy.start()
    barrier = pltpu.get_barrier_semaphore()
    for peer in row_peers + col_peers:
        pl.semaphore_signal(barrier, inc=1, device_id=peer, device_id_type=MESH)

    def near_chip(i):
        return ((x_hi + i // 4) % 2) * 4 + (y + far_fourth(3 - i % 4)) % 4

    def chip_rows(i):
        return pl.ds(pl.multiple_of(near_chip(i) * width, width), width)

    def load(i):
        at = chip_rows(i)
        return pltpu.make_async_copy(s_hbm.at[at], s_f32.at[at], s_sem.at[i])

    def start_load(i, _):
        load(i).start()
        return 0

    lax.fori_loop(0, chips, start_load, 0)

    for copy in small:
        copy.wait()
    lanes = lax.broadcasted_iota(jnp.int32, (4, PAD), 1)
    shift = odd * (PAD - modes)
    mine = (lanes >= shift) & (lanes < shift + modes)
    fresh = jnp.concatenate([b_in[...], width_in[...]], axis=0)
    fresh = jnp.concatenate([fresh, jnp.zeros((4, PAD - modes), F32)], axis=1)
    own_b = jnp.where(odd == 1, pltpu.roll(fresh, PAD - modes, 1), fresh)
    a_slot[col] = own_b
    pl.semaphore_wait(barrier, rows_n + cols_n - 2)

    def send(src, dst, peer, at, arrived=None):
        copy = pltpu.make_async_remote_copy(
            src_ref=src, dst_ref=dst, send_sem=send_sem.at[at],
            recv_sem=recv_sem.at[at] if arrived is None else arrived,
            device_id=peer, device_id_type=MESH)
        copy.start()

    for peer in row_peers:
        send(a_slot.at[col], a_slot.at[col], peer, 0, a_sem.at[col])

    def split(i):
        load(i).wait()

        def some(k, _):
            at = pl.ds(pl.multiple_of(near_chip(i) * width + k * 64, 64), 64)
            whole = s_f32[at]
            high = whole.astype(BF16)
            s_hi[at] = high
            s_lo[at] = (whole - high.astype(F32)).astype(BF16)
            return 0

        lax.fori_loop(0, width // 64, some, 0)

    def turn(i):
        def some(k, _):
            at = pl.ds(pl.multiple_of(near_chip(i) * width + k * LANES, LANES), LANES)
            t_hi[:, at] = s_hi[at].T
            t_lo[:, at] = s_lo[at].T
            return 0

        lax.fori_loop(0, width // LANES, some, 0)

    early = chips // 2

    def prepare(i, _):
        split(i)
        turn(i)
        return 0

    lax.fori_loop(0, early, prepare, 0)

    def first(i, total):
        @pl.when(i >= early)
        def _():
            split(i)

        chip = near_chip(i)
        for j in range(2):
            @pl.when(2 * chip + j != col)
            def _():
                arrived = a_slot.at[2 * chip + j]
                pltpu.make_async_copy(arrived, arrived, a_sem.at[2 * chip + j]).wait()

        left, right = a_slot[2 * chip], a_slot[2 * chip + 1]
        vector = jnp.concatenate([left[:, :LANES], left[:, LANES:] + right[:, :LANES], right[:, LANES:]], axis=1)
        at = chip_rows(i)
        v_buf[:, at] = vector
        part = three_parts(vector)
        total = total + jnp.dot(part, s_hi[at], preferred_element_type=F32)
        return total + jnp.dot(part, s_lo[at], preferred_element_type=F32)

    total = lax.fori_loop(0, chips, first, jnp.zeros((16, block_cols), F32))
    on_diagonal = row == col // 2
    half = v_buf[:, pl.ds(pl.multiple_of(odd * block_cols, LANES), block_cols)]
    flag = jnp.where(on_diagonal, 1.0, 0.0).astype(F32)
    p_slot[row] = joined(total) + half * half[3:4] * flag
    for peer in col_peers:
        send(p_slot.at[row], p_slot.at[row], peer, 1)

    def turn_late(i, _):
        turn(i)
        return 0

    lax.fori_loop(early, chips, turn_late, 0)
    await_bytes(p_slot, rows_n - 1, recv_sem.at[1])
    w1 = p_slot[0]
    for i in range(1, rows_n):
        w1 = w1 + p_slot[i]
    w_buf[...] = w1

    home = col // 2
    away = (z - home // 2) % 4
    across = jnp.where(x_lo == home % 2, 0, 1)
    giving = away < 2
    targets = []
    for j in range(2):
        y_to = (y + jnp.where(away == 0, 2 - j, 3 * j)) % 4
        targets += [(home, ((x_hi + across) % 2) * 8 + y_to * 2 + core) for core in range(2)]

    @pl.when(giving)
    def _():
        for peer in targets:
            send(w_buf, f_slot.at[odd], peer, 2)

    def window(j):
        return pl.ds(pl.multiple_of((j // 2) * width + (j % 2) * LANES, LANES), PAD)

    w_parts = three_parts(w1)
    for i in range(cols_n // 4):
        at = pl.ds(i * 2 * width, 2 * width)
        out = jnp.dot(w_parts, t_hi[:, at], preferred_element_type=F32)
        out = out + jnp.dot(w_parts, t_lo[:, at], preferred_element_type=F32)
        q_buf[:, at] = joined(out)
        for j in range(4):
            to = 4 * i + j

            @pl.when(to != col)
            def _():
                send(q_buf.at[:, window(to)], d_slot.at[col], (row, to), 3)

    d_slot[col] = q_buf[:, window(col)]

    await_bytes(f_slot, 2, recv_sem.at[2])
    per_block = block_cols // modes
    own_w1 = jnp.where(mine, f_slot[col // per_block, :, window(col % per_block)], 0.0)

    def inner(u, v):
        return jnp.sum(u * v, axis=1, keepdims=True)

    cross = jnp.zeros((4, LANES), F32)
    per_half = block_cols // LANES
    for i in range(block_rows // LANES):
        near = f_slot[i // per_half, :, (i % per_half) * LANES:(i % per_half + 1) * LANES]
        cross = cross + near * q_buf[:, i * LANES:(i + 1) * LANES]
    last = jnp.sum(cross, axis=1, keepdims=True) + inner(own_b[3:4] * own_w1, own_w1)
    lane = lax.broadcasted_iota(jnp.int32, (4, LANES), 1)
    table = jnp.zeros((4, LANES), F32)
    for i, moment in enumerate([inner(own_b, own_b), inner(own_b, own_w1), inner(own_w1, own_w1), last]):
        table = jnp.where(lane == i, moment, table)
    line = table[0:1] + pltpu.roll(table[1:2], 4, 1) + pltpu.roll(table[2:3], 8, 1)
    e_slot[pl.ds(me, 1)] = line
    for peer in everyone:
        send(e_slot.at[pl.ds(me, 1)], e_slot.at[pl.ds(me, 1)], peer, 4)

    await_bytes(d_slot, cols_n - 1, recv_sem.at[3])
    w2 = d_slot[0]
    for i in range(1, cols_n):
        w2 = w2 + d_slot[i]
    own_w2 = jnp.where(mine, w2, 0.0) + own_b[3:4] * own_w1

    n = rows_n * cols_n
    await_bytes(e_slot, n - 1, recv_sem.at[4])
    line = jnp.sum(e_slot[...], axis=0, keepdims=True)
    g = jnp.concatenate([line, pltpu.roll(line, LANES - 4, 1), pltpu.roll(line, LANES - 8, 1), line], axis=0)
    g0, g1, g2, g3 = (g[:, i:i + 1] for i in range(4))
    a0 = g0 / g1
    norm = g0 - 2.0 * a0 * g1 + a0 * a0 * g2
    beta = norm / g0
    more = 1.0 + beta
    a1 = norm / (more * more * g1 - 2.0 * more * a0 * g2 + a0 * a0 * g3)
    r1 = own_b - a0 * own_w1
    results = [a0 * own_b + a1 * (r1 + beta * own_b) - r1, r1, a1 * (more * own_w1 - a0 * own_w2)]
    for ref, value in zip((x_part, res_part, res_step), results):
        value = jnp.where(odd == 1, pltpu.roll(value, modes, 1), value)
        ref[...] = value[0:3, :modes]

    await_bytes(a_slot, cols_n - 1, send_sem.at[0])
    await_bytes(p_slot, rows_n - 1, send_sem.at[1])
    await_bytes(d_slot, cols_n - 1, send_sem.at[3])
    await_bytes(e_slot, n - 1, send_sem.at[4])

    @pl.when(giving)
    def _():
        await_bytes(f_slot, 2, send_sem.at[2])
        await_bytes(f_slot, 2, send_sem.at[2])


def solution(mesh):
    rows_n, cols_n = mesh.shape["row"], mesh.shape["col"]
    n = rows_n * cols_n

    def body(right_side, linewidth, scattering):
        block_rows, block_cols = scattering.shape
        vmem, anywhere = pl.BlockSpec(memory_space=pltpu.VMEM), pl.BlockSpec(memory_space=pl.ANY)
        line = linewidth.reshape(1, -1)
        x_part, res_part, res_step = pl.pallas_call(
            functools.partial(kernel, rows_n, cols_n),
            out_shape=(pltpu.VMEM(right_side.shape, F32),) * 3,
            in_specs=[anywhere] * 3,
            out_specs=(vmem,) * 3,
            scratch_shapes=[
                pltpu.VMEM((block_rows, block_cols), F32),
                pltpu.VMEM((block_rows, block_cols), BF16),
                pltpu.VMEM((block_rows, block_cols), BF16),
                pltpu.VMEM((block_cols, block_rows), BF16),
                pltpu.VMEM((block_cols, block_rows), BF16),
                pltpu.VMEM(right_side.shape, F32),
                pltpu.VMEM(line.shape, F32),
                pltpu.VMEM((cols_n, 4, PAD), F32),
                pltpu.VMEM((4, block_rows), F32),
                pltpu.VMEM((rows_n, 4, block_cols), F32),
                pltpu.VMEM((4, block_cols), F32),
                pltpu.VMEM((2, 4, block_cols), F32),
                pltpu.VMEM((4, block_rows), F32),
                pltpu.VMEM((cols_n, 4, PAD), F32),
                pltpu.VMEM((n, LANES), F32),
                pltpu.SemaphoreType.DMA((cols_n // 2,)),
                pltpu.SemaphoreType.DMA((2,)),
                pltpu.SemaphoreType.DMA((cols_n,)),
                pltpu.SemaphoreType.DMA((5,)),
                pltpu.SemaphoreType.DMA((5,)),
            ],
            compiler_params=pltpu.CompilerParams(
                collective_id=0, has_side_effects=True, vmem_limit_bytes=60 << 20),
        )(right_side, line, scattering)
        return x_part + res_part, res_part - res_step

    return jax.shard_map(
        body,
        mesh=mesh,
        in_specs=(P(None, ROW_COL), P(ROW_COL), P("row", "col")),
        out_specs=(P(None, ROW_COL), P(None, ROW_COL)),
        check_vma=False,
    )
```

time: 43.4 us -> 36.7 us (0.85)
  Pallas kernels: 40 us -> 35.3 us
  local copies, waits for them, and re-layouts: 2.53 us -> 0 us
  other arithmetic: 0 us -> 0.6 us
    pallas_call x1, Pallas kernels: 40 us -> 35.3 us  [body(): pl.pallas_call(functools.partial(kernel, rows_n, cols_n), out_shape=(pltp...]
    unnamed x2 -> x0, local copies, waits for them, and re-layouts: 2.53 us -> none
    sub x0 -> x1, other arithmetic: none -> 0.6 us  [body(): return (x_part + res_part, res_part - res_step)]
where the time goes in v2:
time: 36.7 us; the launch traced here: 36.6 us
  Pallas kernels  35.3 us (96%)
  between operations  0.64 us (2%)
  other arithmetic  0.6 us (2%)
    pallas_call x1, Pallas kernels, body(): pl.pallas_call(functools.partial(kernel, rows_n, cols_n), out_shape=(pltp...  35.3 us

profile of v2, /device:TPU:1, one launch (start us, length us, event | category | flops | bytes accessed | tf_op | source)
XLA Modules:
  0.0 36.6 jit_solution(11735489300613842831)
XLA Ops:
  0.6 35.3 %shard_map.50 = (f32[3,192]{1,0:T(4,128)S(1)}, f32[3,192]{1,0:T(4,128)S(1)}, f32[3,192]{1,0:T(4,128)S(1)}) custom-call(f32[3,192]{1,0:T(4,128)} %b_hbm.1, f32[1,192]{1,0:T(1,128)} %bitcast.1, f32[3072,1536]{1,0:T(8,128)} %s_hbm.1), custom_call_target="tpu_custom_call" | custom-call | tf_op jit(solution)/shard_map/pallas_call | solution.py:288
  36.0 0.6 %fusion = (f32[3,192]{1,0:T(4,128)}, f32[3,192]{1,0:T(4,128)}) fusion(f32[3,192]{1,0:T(4,128)S(1)} %get-tuple-element.6, f32[3,192]{1,0:T(4,128)S(1)} %get-tuple-element.7, f32[3,192]{1,0:T(4,128)S(1)} %get-tuple-element.5), kind=kLoop, calls=%fused_computation | loop fusion | flops 1152 | bytes 11520 | tf_op jit(solution)/shard_map/sub | solution.py:318

commit v3 on v2

--- a/solution.py
+++ b/solution.py
@@ -11,6 +11,8 @@
 MESH = pl.DeviceIdType.MESH
 F32, BF16 = jnp.float32, jnp.bfloat16
 LANES = 128
+TURNED = 5
+FAR = 44
 PAD = 2 * LANES
 
 
@@ -133,29 +135,18 @@
 
         lax.fori_loop(0, width // 64, some, 0)
 
-    def turn(i):
-        def some(k, _):
-            at = pl.ds(pl.multiple_of(near_chip(i) * width + k * LANES, LANES), LANES)
-            t_hi[:, at] = s_hi[at].T
-            t_lo[:, at] = s_lo[at].T
-            return 0
-
-        lax.fori_loop(0, width // LANES, some, 0)
-
     early = chips // 2
 
     def prepare(i, _):
         split(i)
-        turn(i)
         return 0
 
     lax.fori_loop(0, early, prepare, 0)
 
-    def first(i, total):
-        @pl.when(i >= early)
-        def _():
+    total = jnp.zeros((16, block_cols), F32)
+    for i in range(chips):
+        if i >= early:
             split(i)
-
         chip = near_chip(i)
         for j in range(2):
             @pl.when(2 * chip + j != col)
@@ -169,9 +160,7 @@
         v_buf[:, at] = vector
         part = three_parts(vector)
         total = total + jnp.dot(part, s_hi[at], preferred_element_type=F32)
-        return total + jnp.dot(part, s_lo[at], preferred_element_type=F32)
-
-    total = lax.fori_loop(0, chips, first, jnp.zeros((16, block_cols), F32))
+        total = total + jnp.dot(part, s_lo[at], preferred_element_type=F32)
     on_diagonal = row == col // 2
     half = v_buf[:, pl.ds(pl.multiple_of(odd * block_cols, LANES), block_cols)]
     flag = jnp.where(on_diagonal, 1.0, 0.0).astype(F32)
@@ -179,11 +168,17 @@
     for peer in col_peers:
         send(p_slot.at[row], p_slot.at[row], peer, 1)
 
-    def turn_late(i, _):
-        turn(i)
+    turned = t_hi.shape[1]
+    per_chip = width // LANES
+
+    def turn(i, _):
+        rows = pl.ds(pl.multiple_of(near_chip(i // per_chip) * width + (i % per_chip) * LANES, LANES), LANES)
+        at = pl.ds(pl.multiple_of(i * LANES, LANES), LANES)
+        t_hi[:, at] = s_hi[rows].T
+        t_lo[:, at] = s_lo[rows].T
         return 0
 
-    lax.fori_loop(early, chips, turn_late, 0)
+    lax.fori_loop(0, turned // LANES, turn, 0)
     await_bytes(p_slot, rows_n - 1, recv_sem.at[1])
     w1 = p_slot[0]
     for i in range(1, rows_n):
@@ -208,18 +203,16 @@
         return pl.ds(pl.multiple_of((j // 2) * width + (j % 2) * LANES, LANES), PAD)
 
     w_parts = three_parts(w1)
-    for i in range(cols_n // 4):
-        at = pl.ds(i * 2 * width, 2 * width)
-        out = jnp.dot(w_parts, t_hi[:, at], preferred_element_type=F32)
-        out = out + jnp.dot(w_parts, t_lo[:, at], preferred_element_type=F32)
-        q_buf[:, at] = joined(out)
-        for j in range(4):
-            to = 4 * i + j
-
-            @pl.when(to != col)
-            def _():
-                send(q_buf.at[:, window(to)], d_slot.at[col], (row, to), 3)
-
+    near = jnp.dot(w_parts, t_hi[...], preferred_element_type=F32)
+    near = joined(near + jnp.dot(w_parts, t_lo[...], preferred_element_type=F32))
+    for i in range(chips):
+        at = chip_rows(i)
+        if (i + 1) * width <= turned:
+            q_buf[:, at] = near[:, i * width:(i + 1) * width]
+        else:
+            dims = (((1,), (1,)), ((), ()))
+            out = lax.dot_general(w_parts, s_hi[at], dims, preferred_element_type=F32)
+            q_buf[:, at] = joined(out + lax.dot_general(w_parts, s_lo[at], dims, preferred_element_type=F32))
     d_slot[col] = q_buf[:, window(col)]
 
     await_bytes(f_slot, 2, recv_sem.at[2])
@@ -232,8 +225,8 @@
     cross = jnp.zeros((4, LANES), F32)
     per_half = block_cols // LANES
     for i in range(block_rows // LANES):
-        near = f_slot[i // per_half, :, (i % per_half) * LANES:(i % per_half + 1) * LANES]
-        cross = cross + near * q_buf[:, i * LANES:(i + 1) * LANES]
+        part = f_slot[i // per_half, :, (i % per_half) * LANES:(i % per_half + 1) * LANES]
+        cross = cross + part * q_buf[:, i * LANES:(i + 1) * LANES]
     last = jnp.sum(cross, axis=1, keepdims=True) + inner(own_b[3:4] * own_w1, own_w1)
     lane = lax.broadcasted_iota(jnp.int32, (4, LANES), 1)
     table = jnp.zeros((4, LANES), F32)
@@ -241,8 +234,15 @@
         table = jnp.where(lane == i, moment, table)
     line = table[0:1] + pltpu.roll(table[1:2], 4, 1) + pltpu.roll(table[2:3], 8, 1)
     e_slot[pl.ds(me, 1)] = line
-    for peer in everyone:
-        send(e_slot.at[pl.ds(me, 1)], e_slot.at[pl.ds(me, 1)], peer, 4)
+
+    def tell(peers):
+        for peer in peers:
+            send(e_slot.at[pl.ds(me, 1)], e_slot.at[pl.ds(me, 1)], peer, 4)
+
+    tell(everyone[:FAR])
+    for to_row, to_col in row_peers:
+        send(q_buf.at[:, window(to_col)], d_slot.at[col], (to_row, to_col), 3)
+    tell(everyone[FAR:])
 
     await_bytes(d_slot, cols_n - 1, recv_sem.at[3])
     w2 = d_slot[0]
@@ -294,8 +294,8 @@
                 pltpu.VMEM((block_rows, block_cols), F32),
                 pltpu.VMEM((block_rows, block_cols), BF16),
                 pltpu.VMEM((block_rows, block_cols), BF16),
-                pltpu.VMEM((block_cols, block_rows), BF16),
-                pltpu.VMEM((block_cols, block_rows), BF16),
+                pltpu.VMEM((block_cols, block_rows // 8 * TURNED), BF16),
+                pltpu.VMEM((block_cols, block_rows // 8 * TURNED), BF16),
                 pltpu.VMEM(right_side.shape, F32),
                 pltpu.VMEM(line.shape, F32),
                 pltpu.VMEM((cols_n, 4, PAD), F32),

time: 36.7 us -> 33 us (0.90)
  Pallas kernels: 35.3 us -> 31.6 us
    pallas_call x1, Pallas kernels: 35.3 us -> 31.6 us  [body(): pl.pallas_call(functools.partial(kernel, rows_n, cols_n), out_shape=(pltp...]
where the time goes in v3:
time: 33 us; the launch traced here: 32.9 us
  Pallas kernels  31.6 us (96%)
  between operations  0.64 us (2%)
  other arithmetic  0.6 us (2%)
    pallas_call x1, Pallas kernels, body(): pl.pallas_call(functools.partial(kernel, rows_n, cols_n), out_shape=(pltp...  31.6 us

profile of v3, /device:TPU:1, one launch (start us, length us, event | category | flops | bytes accessed | tf_op | source)
XLA Modules:
  0.0 32.9 jit_solution(7004070253674482539)
XLA Ops:
  0.6 31.6 %shard_map.50 = (f32[3,192]{1,0:T(4,128)S(1)}, f32[3,192]{1,0:T(4,128)S(1)}, f32[3,192]{1,0:T(4,128)S(1)}) custom-call(f32[3,192]{1,0:T(4,128)} %b_hbm.1, f32[1,192]{1,0:T(1,128)} %bitcast.1, f32[3072,1536]{1,0:T(8,128)} %s_hbm.1), custom_call_target="tpu_custom_call" | custom-call | tf_op jit(solution)/shard_map/pallas_call | solution.py:288
  32.3 0.6 %fusion = (f32[3,192]{1,0:T(4,128)}, f32[3,192]{1,0:T(4,128)}) fusion(f32[3,192]{1,0:T(4,128)S(1)} %get-tuple-element.6, f32[3,192]{1,0:T(4,128)S(1)} %get-tuple-element.7, f32[3,192]{1,0:T(4,128)S(1)} %get-tuple-element.5), kind=kLoop, calls=%fused_computation | loop fusion | flops 1152 | bytes 11520 | tf_op jit(solution)/shard_map/sub | solution.py:318

commit v4 on v3

--- a/solution.py
+++ b/solution.py
@@ -186,18 +186,10 @@
     w_buf[...] = w1
 
     home = col // 2
-    away = (z - home // 2) % 4
+    y_to = (y + 2 - z + home // 2) % 4
     across = jnp.where(x_lo == home % 2, 0, 1)
-    giving = away < 2
-    targets = []
-    for j in range(2):
-        y_to = (y + jnp.where(away == 0, 2 - j, 3 * j)) % 4
-        targets += [(home, ((x_hi + across) % 2) * 8 + y_to * 2 + core) for core in range(2)]
-
-    @pl.when(giving)
-    def _():
-        for peer in targets:
-            send(w_buf, f_slot.at[odd], peer, 2)
+    for core in range(2):
+        send(w_buf, f_slot.at[odd], (home, ((x_hi + across) % 2) * 8 + y_to * 2 + core), 2)
 
     def window(j):
         return pl.ds(pl.multiple_of((j // 2) * width + (j % 2) * LANES, LANES), PAD)
@@ -271,10 +263,7 @@
     await_bytes(d_slot, cols_n - 1, send_sem.at[3])
     await_bytes(e_slot, n - 1, send_sem.at[4])
 
-    @pl.when(giving)
-    def _():
-        await_bytes(f_slot, 2, send_sem.at[2])
-        await_bytes(f_slot, 2, send_sem.at[2])
+    await_bytes(f_slot, 2, send_sem.at[2])
 
 
 def solution(mesh):

time: 33 us -> 32.4 us (0.982)
  Pallas kernels: 31.6 us -> 31.1 us
    pallas_call x1, Pallas kernels: 31.6 us -> 31.1 us  [body(): pl.pallas_call(functools.partial(kernel, rows_n, cols_n), out_shape=(pltp...]
where the time goes in v4:
time: 32.4 us; the launch traced here: 32.3 us
  Pallas kernels  31.1 us (96%)
  between operations  0.64 us (2%)
  other arithmetic  0.6 us (2%)
    pallas_call x1, Pallas kernels, body(): pl.pallas_call(functools.partial(kernel, rows_n, cols_n), out_shape=(pltp...  31.1 us

profile of v4, /device:TPU:1, one launch (start us, length us, event | category | flops | bytes accessed | tf_op | source)
XLA Modules:
  0.0 32.3 jit_solution(12957582651071968279)
XLA Ops:
  0.6 31.1 %shard_map.50 = (f32[3,192]{1,0:T(4,128)S(1)}, f32[3,192]{1,0:T(4,128)S(1)}, f32[3,192]{1,0:T(4,128)S(1)}) custom-call(f32[3,192]{1,0:T(4,128)} %b_hbm.1, f32[1,192]{1,0:T(1,128)} %bitcast.1, f32[3072,1536]{1,0:T(8,128)} %s_hbm.1), custom_call_target="tpu_custom_call" | custom-call | tf_op jit(solution)/shard_map/pallas_call | solution.py:277
  31.7 0.6 %fusion = (f32[3,192]{1,0:T(4,128)}, f32[3,192]{1,0:T(4,128)}) fusion(f32[3,192]{1,0:T(4,128)S(1)} %get-tuple-element.6, f32[3,192]{1,0:T(4,128)S(1)} %get-tuple-element.7, f32[3,192]{1,0:T(4,128)S(1)} %get-tuple-element.5), kind=kLoop, calls=%fused_computation | loop fusion | flops 1152 | bytes 11520 | tf_op jit(solution)/shard_map/sub | solution.py:307

commit v5 on v4

--- a/solution.py
+++ b/solution.py
@@ -55,35 +55,25 @@
     modes = b_in.shape[1]
     chips = cols_n // 2
     width = 2 * modes
-    odd = col % 2
-
-    z, x_lo, x_hi, y = row // 2, row % 2, col // 8, (col // 2) % 4
+    odd = lax.rem(col, 2)
+
+    z, x_lo, x_hi, y = row // 2, lax.rem(row, 2), col // 8, lax.rem(col // 2, 4)
     x = x_hi * 2 + x_lo
-    z_at = [((z + d) % 4) * 2 for d in range(4)]
-    y_at = [((y + d) % 4) * 2 for d in range(4)]
-    x_row = [((x + d) % 4) % 2 for d in range(4)]
-    x_col = [((x + d) % 4) // 2 * 8 for d in range(4)]
+    z_at = [lax.rem(z + d, 4) * 2 for d in range(4)]
+    y_at = [lax.rem(y + d, 4) * 2 for d in range(4)]
+    x_hi_at = [x_hi * 8, 8 - x_hi * 8]
     core_at = [odd, 1 - odd]
 
-    def device(offset):
-        dz, dy, dx, dc = offset
-        return (z_at[dz] + x_row[dx], x_col[dx] + y_at[dy] + core_at[dc])
-
-    def col_device(offset):
-        dz, _, dx, _ = offset
-        return (z_at[dz] + (row + dx) % 2, col)
-
-    row_peers = [device(o) for o in farthest_first([(0, dy, dx, dc) for dy in range(4) for dx in (0, 2) for dc in (0, 1)])]
-    col_peers = [col_device(o) for o in farthest_first([(dz, 0, dx, 0) for dz in range(4) for dx in (0, 1)])]
-    everyone = [device(o) for o in farthest_first(
-        [(dz, dy, dx, dc) for dz in range(4) for dy in range(4) for dx in range(4) for dc in (0, 1)])]
-
+    row_peers = [(row, x_hi_at[dx // 2] + y_at[dy] + core_at[dc]) for _, dy, dx, dc in
+                 farthest_first([(0, dy, dx, dc) for dy in range(4) for dx in (0, 2) for dc in (0, 1)])]
+    col_peers = [(z_at[dz] + (1 - x_lo if dx else x_lo), col) for dz, _, dx, _ in
+                 farthest_first([(dz, 0, dx, 0) for dz in range(4) for dx in (0, 1)])]
+    barrier = pltpu.get_barrier_semaphore()
+    for peer in row_peers + col_peers:
+        pl.semaphore_signal(barrier, inc=1, device_id=peer, device_id_type=MESH)
     small = [pltpu.make_async_copy(b_hbm, b_in, in_sem.at[0]), pltpu.make_async_copy(width_hbm, width_in, in_sem.at[1])]
     for copy in small:
         copy.start()
-    barrier = pltpu.get_barrier_semaphore()
-    for peer in row_peers + col_peers:
-        pl.semaphore_signal(barrier, inc=1, device_id=peer, device_id_type=MESH)
 
     def near_chip(i):
         return ((x_hi + i // 4) % 2) * 4 + (y + far_fourth(3 - i % 4)) % 4
@@ -126,16 +116,16 @@
         load(i).wait()
 
         def some(k, _):
-            at = pl.ds(pl.multiple_of(near_chip(i) * width + k * 64, 64), 64)
+            at = pl.ds(pl.multiple_of(near_chip(i) * width + k * 192, 192), 192)
             whole = s_f32[at]
             high = whole.astype(BF16)
             s_hi[at] = high
             s_lo[at] = (whole - high.astype(F32)).astype(BF16)
             return 0
 
-        lax.fori_loop(0, width // 64, some, 0)
-
-    early = chips // 2
+        lax.fori_loop(0, width // 192, some, 0)
+
+    early = chips - 1
 
     def prepare(i, _):
         split(i)
@@ -227,6 +217,12 @@
     line = table[0:1] + pltpu.roll(table[1:2], 4, 1) + pltpu.roll(table[2:3], 8, 1)
     e_slot[pl.ds(me, 1)] = line
 
+    x_at = [lax.rem(x + d, 4) for d in range(4)]
+    x_row = [lax.rem(at, 2) for at in x_at]
+    x_col = [at // 2 * 8 for at in x_at]
+    everyone = [(z_at[dz] + x_row[dx], x_col[dx] + y_at[dy] + core_at[dc]) for dz, dy, dx, dc in farthest_first(
+        [(dz, dy, dx, dc) for dz in range(4) for dy in range(4) for dx in range(4) for dc in (0, 1)])]
+
     def tell(peers):
         for peer in peers:
             send(e_slot.at[pl.ds(me, 1)], e_slot.at[pl.ds(me, 1)], peer, 4)
@@ -241,6 +237,8 @@
     for i in range(1, cols_n):
         w2 = w2 + d_slot[i]
     own_w2 = jnp.where(mine, w2, 0.0) + own_b[3:4] * own_w1
+    own_b, own_w1, own_w2 = (
+        jnp.where(odd == 1, pltpu.roll(value, modes, 1), value)[:, :modes] for value in (own_b, own_w1, own_w2))
 
     n = rows_n * cols_n
     await_bytes(e_slot, n - 1, recv_sem.at[4])
@@ -255,8 +253,7 @@
     r1 = own_b - a0 * own_w1
     results = [a0 * own_b + a1 * (r1 + beta * own_b) - r1, r1, a1 * (more * own_w1 - a0 * own_w2)]
     for ref, value in zip((x_part, res_part, res_step), results):
-        value = jnp.where(odd == 1, pltpu.roll(value, modes, 1), value)
-        ref[...] = value[0:3, :modes]
+        ref[...] = value[0:3]
 
     await_bytes(a_slot, cols_n - 1, send_sem.at[0])
     await_bytes(p_slot, rows_n - 1, send_sem.at[1])

time: 32.4 us -> 31.7 us (0.978)
  Pallas kernels: 31.1 us -> 30.4 us
    pallas_call x1, Pallas kernels: 31.1 us -> 30.4 us  [body(): pl.pallas_call(functools.partial(kernel, rows_n, cols_n), out_shape=(pltp...]
where the time goes in v5:
time: 31.7 us; the launch traced here: 31.6 us
  Pallas kernels  30.4 us (96%)
  between operations  0.64 us (2%)
  other arithmetic  0.6 us (2%)
    pallas_call x1, Pallas kernels, body(): pl.pallas_call(functools.partial(kernel, rows_n, cols_n), out_shape=(pltp...  30.4 us

profile of v5, /device:TPU:1, one launch (start us, length us, event | category | flops | bytes accessed | tf_op | source)
XLA Modules:
  0.0 31.6 jit_solution(7178704611946029723)
XLA Ops:
  0.6 30.4 %shard_map.50 = (f32[3,192]{1,0:T(4,128)S(1)}, f32[3,192]{1,0:T(4,128)S(1)}, f32[3,192]{1,0:T(4,128)S(1)}) custom-call(f32[3,192]{1,0:T(4,128)} %b_hbm.1, f32[1,192]{1,0:T(1,128)} %bitcast.1, f32[3072,1536]{1,0:T(8,128)} %s_hbm.1), custom_call_target="tpu_custom_call" | custom-call | tf_op jit(solution)/shard_map/pallas_call | solution.py:274
  31.0 0.6 %fusion = (f32[3,192]{1,0:T(4,128)}, f32[3,192]{1,0:T(4,128)}) fusion(f32[3,192]{1,0:T(4,128)S(1)} %get-tuple-element.6, f32[3,192]{1,0:T(4,128)S(1)} %get-tuple-element.7, f32[3,192]{1,0:T(4,128)S(1)} %get-tuple-element.5), kind=kLoop, calls=%fused_computation | loop fusion | flops 1152 | bytes 11520 | tf_op jit(solution)/shard_map/sub | solution.py:304

commit v6 on v5

--- a/solution.py
+++ b/solution.py
@@ -11,6 +11,7 @@
 MESH = pl.DeviceIdType.MESH
 F32, BF16 = jnp.float32, jnp.bfloat16
 LANES = 128
+SPLIT_BEFORE = {1: (5,), 3: (6,), 5: (7,)}
 TURNED = 5
 FAR = 44
 PAD = 2 * LANES
@@ -125,7 +126,7 @@
 
         lax.fori_loop(0, width // 192, some, 0)
 
-    early = chips - 1
+    early = chips - 3
 
     def prepare(i, _):
         split(i)
@@ -135,8 +136,8 @@
 
     total = jnp.zeros((16, block_cols), F32)
     for i in range(chips):
-        if i >= early:
-            split(i)
+        for late in SPLIT_BEFORE.get(i, ()):
+            split(late)
         chip = near_chip(i)
         for j in range(2):
             @pl.when(2 * chip + j != col)

time: 31.7 us -> 31.4 us (level)
    pallas_call x1, Pallas kernels: 30.4 us -> 30.1 us  [body(): pl.pallas_call(functools.partial(kernel, rows_n, cols_n), out_shape=(pltp...]
where the time goes in v6:
time: 31.4 us; the launch traced here: 31.3 us
  Pallas kernels  30.1 us (96%)
  between operations  0.64 us (2%)
  other arithmetic  0.6 us (2%)
    pallas_call x1, Pallas kernels, body(): pl.pallas_call(functools.partial(kernel, rows_n, cols_n), out_shape=(pltp...  30.1 us

profile of v6, /device:TPU:1, one launch (start us, length us, event | category | flops | bytes accessed | tf_op | source)
XLA Modules:
  0.0 31.3 jit_solution(2176937601340529768)
XLA Ops:
  0.6 30.1 %shard_map.50 = (f32[3,192]{1,0:T(4,128)S(1)}, f32[3,192]{1,0:T(4,128)S(1)}, f32[3,192]{1,0:T(4,128)S(1)}) custom-call(f32[3,192]{1,0:T(4,128)} %b_hbm.1, f32[1,192]{1,0:T(1,128)} %bitcast.1, f32[3072,1536]{1,0:T(8,128)} %s_hbm.1), custom_call_target="tpu_custom_call" | custom-call | tf_op jit(solution)/shard_map/pallas_call | solution.py:275
  30.7 0.6 %fusion = (f32[3,192]{1,0:T(4,128)}, f32[3,192]{1,0:T(4,128)}) fusion(f32[3,192]{1,0:T(4,128)S(1)} %get-tuple-element.6, f32[3,192]{1,0:T(4,128)S(1)} %get-tuple-element.7, f32[3,192]{1,0:T(4,128)S(1)} %get-tuple-element.5), kind=kLoop, calls=%fused_computation | loop fusion | flops 1152 | bytes 11520 | tf_op jit(solution)/shard_map/sub | solution.py:305

commit v7 on v6

--- a/solution.py
+++ b/solution.py
@@ -11,7 +11,7 @@
 MESH = pl.DeviceIdType.MESH
 F32, BF16 = jnp.float32, jnp.bfloat16
 LANES = 128
-SPLIT_BEFORE = {1: (5,), 3: (6,), 5: (7,)}
+SPLIT_BEFORE = {1: (4,), 2: (5,), 3: (6,), 5: (7,)}
 TURNED = 5
 FAR = 44
 PAD = 2 * LANES
@@ -126,7 +126,7 @@
 
         lax.fori_loop(0, width // 192, some, 0)
 
-    early = chips - 3
+    early = chips - 4
 
     def prepare(i, _):
         split(i)

time: 31.4 us -> 31.6 us (level)
  no operation moved by 1% of the time
where the time goes in v7:
time: 31.6 us; the launch traced here: 31.5 us
  Pallas kernels  30.2 us (96%)
  between operations  0.64 us (2%)
  other arithmetic  0.6 us (2%)
    pallas_call x1, Pallas kernels, body(): pl.pallas_call(functools.partial(kernel, rows_n, cols_n), out_shape=(pltp...  30.2 us

profile of v7, /device:TPU:1, one launch (start us, length us, event | category | flops | bytes accessed | tf_op | source)
XLA Modules:
  0.0 31.5 jit_solution(10548593237726355952)
XLA Ops:
  0.6 30.2 %shard_map.50 = (f32[3,192]{1,0:T(4,128)S(1)}, f32[3,192]{1,0:T(4,128)S(1)}, f32[3,192]{1,0:T(4,128)S(1)}) custom-call(f32[3,192]{1,0:T(4,128)} %b_hbm.1, f32[1,192]{1,0:T(1,128)} %bitcast.1, f32[3072,1536]{1,0:T(8,128)} %s_hbm.1), custom_call_target="tpu_custom_call" | custom-call | tf_op jit(solution)/shard_map/pallas_call | solution.py:275
  30.9 0.6 %fusion = (f32[3,192]{1,0:T(4,128)}, f32[3,192]{1,0:T(4,128)}) fusion(f32[3,192]{1,0:T(4,128)S(1)} %get-tuple-element.6, f32[3,192]{1,0:T(4,128)S(1)} %get-tuple-element.7, f32[3,192]{1,0:T(4,128)S(1)} %get-tuple-element.5), kind=kLoop, calls=%fused_computation | loop fusion | flops 1152 | bytes 11520 | tf_op jit(solution)/shard_map/sub | solution.py:305
